TPU v7x, 32 devices: a whole 2x2x4 slice. The times are simulated.
32 devices in a mesh: fsdp: 4 (over x, core), ctx: 2 (over y), tp: 4 (over z).
Axes of the slice: x: 2, y: 2, z: 4, core: 2. Of those that a mesh axis runs over, the one named last changes fastest.
Arguments:
- tokens: bfloat16 [8, 1024, 768], P('fsdp', 'ctx'), may hold values from -6 to 6
- segments: int32 [8, 1024], P('fsdp', 'ctx'), may hold values from 0 to 3, never falling along the last dimension, each value on 1 to 768 neighbouring positions
- ln_gains: bfloat16 [2, 768], P(None, 'fsdp'), may hold values from 0.5 to 1.5
- ln_biases: bfloat16 [2, 768], P(None, 'fsdp'), may hold values from -1.75 to 1.75
- w_qkv: bfloat16 [3, 768, 768], P(None, 'fsdp', 'tp'), may hold values from -0.21875 to 0.21875
- bias_qv: bfloat16 [2, 12, 64], P(None, 'tp', 'fsdp'), may hold values from -3 to 3
- w_out: bfloat16 [768, 768], P('tp', 'fsdp'), may hold values from -1.25 to 1.25
- out_biases: bfloat16 [2, 768], P(None, 'fsdp'), may hold values from -1.75 to 1.75
- w_up: bfloat16 [768, 3072], P('fsdp', 'tp'), may hold values from -0.21875 to 0.21875
- up_bias: bfloat16 [48, 64], P('tp', 'fsdp'), may hold values from -3 to 3
- w_down: bfloat16 [3072, 768], P('tp', 'fsdp'), may hold values from -0.109375 to 0.109375
- cotangent: bfloat16 [8, 1024, 768], P('fsdp', 'ctx'), may hold values from -6 to 6
Outputs:
- output: bfloat16 [8, 1024, 768], P('fsdp', 'ctx')
- grad_tokens: float32 [8, 1024, 768], P('fsdp', 'ctx')
- grad_ln_gains: float32 [2, 768], P(None, 'fsdp')
- grad_ln_biases: float32 [2, 768], P(None, 'fsdp')
- grad_qkv: float32 [3, 768, 768], P(None, 'fsdp', 'tp')
- grad_bias_qv: float32 [2, 12, 64], P(None, 'tp', 'fsdp')
- grad_out_proj: float32 [768, 768], P('tp', 'fsdp')
- grad_out_biases: float32 [2, 768], P(None, 'fsdp')
- grad_up: float32 [768, 3072], P('fsdp', 'tp')
- grad_up_bias: float32 [48, 64], P('tp', 'fsdp')
- grad_down: float32 [3072, 768], P('tp', 'fsdp')
Inputs may be any that keep to these rules, and one draw needn't show every extreme that they name: `segments`: within each sequence the numbers never fall; each document holds 1 to 768 positions, and one document of each sequence exactly that many.
All inputs are finite; a program needn't handle non-finite values.
Results may differ from a plain program's by a relative error of at most 0.017.
Values may be sent and summed in bfloat16 or wider, within the bound.
No kernel may reach another device: no remote copies, remote signals or barrier semaphores. Data moves between devices by JAX's collectives and lax.ppermute only.
A program may use at most 384 MiB of HBM per device.

v0:
```python
import jax
import jax.numpy as jnp
from jax import lax
from jax.sharding import PartitionSpec as P

HD = 64
eps = 1e-05
masked_score = -1e30


def layer_norm(values_in, gain, shift):
    average = jnp.mean(values_in, axis=-1, keepdims=True)
    centered = values_in - average
    variance = jnp.mean(centered * centered, axis=-1, keepdims=True)
    return centered * lax.rsqrt(variance + eps) * gain + shift


def gelu_tanh(values_in):
    return jax.nn.gelu(values_in, approximate=True)


def block_scores(queries, key_rows, query_place, query_doc, key_place, key_doc):
    scores = (
        jnp.einsum("qhd,khd->hqk", queries, key_rows, preferred_element_type=jnp.float32) * 0.125
    )
    allowed = (query_doc[:, None] == key_doc[None, :]) & (
        key_place[None, :] <= query_place[:, None]
    )
    return jnp.where(allowed[None], scores, masked_score)


def tp_total(make, row_count):
    return lax.psum(make(0, row_count), "tp")


def local(
    tokens,
    segments,
    ln_gains,
    ln_biases,
    w_qkv,
    bias_qv,
    w_out,
    out_biases,
    w_up,
    up_bias,
    w_down,
    cotangent,
):
    gathered = (
        lax.all_gather(ln_gains, "fsdp", axis=1, tiled=True),
        lax.all_gather(ln_biases, "fsdp", axis=1, tiled=True),
        lax.all_gather(w_qkv, "fsdp", axis=1, tiled=True),
        lax.all_gather(bias_qv, "fsdp", axis=2, tiled=True),
        lax.all_gather(w_out, "fsdp", axis=1, tiled=True),
        lax.all_gather(out_biases, "fsdp", axis=1, tiled=True),
        lax.all_gather(w_up, "fsdp", axis=0, tiled=True),
        lax.all_gather(up_bias, "fsdp", axis=1, tiled=True),
        lax.all_gather(w_down, "fsdp", axis=1, tiled=True),
    )
    (
        gain_rows,
        shift_rows,
        qkv_proj,
        qv_bias,
        out_proj,
        branch_bias,
        up_proj,
        up_shift,
        down_proj,
    ) = gathered
    gain_rows = gain_rows.astype(jnp.float32)
    shift_rows = shift_rows.astype(jnp.float32)
    branch_bias = branch_bias.astype(jnp.float32)
    seq_count, block_len, width = tokens.shape
    row_count = seq_count * block_len
    width_heads = qkv_proj.shape[2]
    head_count = width_heads // HD
    inputs = tokens.astype(jnp.float32).reshape(row_count, width)
    cot_rows = cotangent.reshape(row_count, width)
    normed_low = layer_norm(inputs, gain_rows[0], shift_rows[0]).astype(jnp.bfloat16)
    projected = jnp.einsum("td,cdh->cth", normed_low, qkv_proj, preferred_element_type=jnp.float32)
    bias_flat = qv_bias.astype(jnp.float32).reshape(2, width_heads)
    query_low = (projected[0] + bias_flat[0]).astype(jnp.bfloat16)
    key_low = projected[1].astype(jnp.bfloat16)
    value_low = (projected[2] + bias_flat[1]).astype(jnp.bfloat16)
    pair_local = jnp.concatenate([key_low, value_low], axis=1).reshape(
        seq_count, block_len, 2 * width_heads
    )
    pair_rows, doc_rows = (
        lax.all_gather(pair_local, "ctx", axis=1, tiled=True),
        lax.all_gather(segments.astype(jnp.bfloat16), "ctx", axis=1, tiled=True),
    )
    full_len = pair_rows.shape[1]
    key_rows = pair_rows[:, :, :width_heads].reshape(seq_count, full_len, head_count, HD)
    value_rows = pair_rows[:, :, width_heads:].reshape(seq_count, full_len, head_count, HD)
    key_doc = doc_rows.astype(jnp.float32)
    key_place = jnp.arange(full_len, dtype=jnp.int32)
    block_rows = min(512, block_len)
    block_count = block_len // block_rows
    query_place = (
        lax.axis_index("ctx") * block_len + jnp.arange(block_len, dtype=jnp.int32)
    ).reshape(block_count, block_rows)
    query_doc = segments.astype(jnp.float32).reshape(seq_count, block_count, block_rows)
    query_blocks = query_low.reshape(seq_count, block_count, block_rows, head_count, HD)

    def forward_sequence(seq_item):
        seq_queries, seq_keys, seq_values, seq_key_doc, seq_query_doc = seq_item

        def forward_block(block_item):
            queries, places, doc_ids = block_item
            scores = block_scores(queries, seq_keys, places, doc_ids, key_place, seq_key_doc)
            row_max = jnp.max(scores, axis=-1, keepdims=True)
            exponent = jnp.exp(scores - row_max)
            totals = jnp.sum(exponent, axis=-1, keepdims=True)
            probability = (exponent / totals).astype(jnp.bfloat16)
            mixture = jnp.einsum(
                "hqk,khd->qhd", probability, seq_values, preferred_element_type=jnp.float32
            )
            return (mixture, (row_max + jnp.log(totals))[..., 0])

        return lax.map(forward_block, (seq_queries, query_place, seq_query_doc))

    mixture, log_sums = lax.map(
        forward_sequence, (query_blocks, key_rows, value_rows, key_doc, query_doc)
    )
    attended_low = mixture.reshape(row_count, width_heads).astype(jnp.bfloat16)

    def make_attn(start, count):
        return jnp.dot(attended_low, out_proj, preferred_element_type=jnp.float32)

    branch_part = tp_total(make_attn, row_count)
    hidden = inputs + branch_part + branch_bias[0]
    normed_two, norm_two_pull = jax.vjp(layer_norm, hidden, gain_rows[1], shift_rows[1])
    normed_two_own = normed_two.astype(jnp.bfloat16)
    pre_act = jnp.dot(
        normed_two_own, up_proj, preferred_element_type=jnp.float32
    ) + up_shift.astype(jnp.float32).reshape(-1)
    activated, gelu_pull = jax.vjp(gelu_tanh, pre_act)
    activated_low = activated.astype(jnp.bfloat16)

    def make_down(start, count):
        return jnp.dot(activated_low, down_proj, preferred_element_type=jnp.float32)

    second = tp_total(make_down, row_count) + branch_bias[1]
    result_own = (hidden + second).astype(jnp.bfloat16)
    qkv_back, out_back, up_back, down_back = (
        lax.all_gather(w_qkv, "fsdp", axis=1, tiled=True),
        lax.all_gather(w_out, "fsdp", axis=1, tiled=True),
        lax.all_gather(w_up, "fsdp", axis=0, tiled=True),
        lax.all_gather(w_down, "fsdp", axis=1, tiled=True),
    )
    grad_act_low = jnp.einsum(
        "td,fd->tf", cot_rows, down_back, preferred_element_type=jnp.float32
    ).astype(jnp.bfloat16)
    (grad_pre,) = gelu_pull(grad_act_low.astype(jnp.float32))
    grad_pre_low = grad_pre.astype(jnp.bfloat16)
    grad_down = jnp.einsum("tf,td->fd", activated_low, cot_rows, preferred_element_type=jnp.float32)
    grad_up = jnp.einsum(
        "td,tf->df", normed_two_own, grad_pre_low, preferred_element_type=jnp.float32
    )
    grad_up_bias = jnp.sum(grad_pre_low.astype(jnp.float32), axis=0).reshape(up_shift.shape)

    def make_mlp_back(start, count):
        return jnp.einsum("tf,df->td", grad_pre_low, up_back, preferred_element_type=jnp.float32)

    grad_normed_two = tp_total(make_mlp_back, row_count)
    grad_hidden_norm, grad_gain_two, grad_shift_two = norm_two_pull(grad_normed_two)
    grad_hidden = cot_rows.astype(jnp.float32) + grad_hidden_norm
    grad_branch_own = grad_hidden.astype(jnp.bfloat16)
    grad_out_proj = jnp.einsum(
        "th,td->hd", attended_low, grad_branch_own, preferred_element_type=jnp.float32
    )
    grad_attended = jnp.einsum(
        "td,hd->th", grad_branch_own, out_back, preferred_element_type=jnp.float32
    ).astype(jnp.bfloat16)
    grad_blocks = grad_attended.reshape(seq_count, block_count, block_rows, head_count, HD)

    def backward_sequence(seq_item):
        seq_queries, seq_grads, seq_logs, seq_keys, seq_values, seq_key_doc, seq_query_doc = (
            seq_item
        )

        def backward_block(running, block_item):
            key_sum, value_sum = running
            queries, grad_rows, log_sum, places, doc_ids = block_item
            scores = block_scores(queries, seq_keys, places, doc_ids, key_place, seq_key_doc)
            probability = jnp.exp(scores - log_sum[..., None])
            grad_prob = jnp.einsum(
                "qhd,khd->hqk", grad_rows, seq_values, preferred_element_type=jnp.float32
            )
            inner_sum = jnp.sum(probability * grad_prob, axis=-1, keepdims=True)
            grad_scores = (probability * (grad_prob - inner_sum) * 0.125).astype(jnp.bfloat16)
            grad_query = jnp.einsum(
                "hqk,khd->qhd", grad_scores, seq_keys, preferred_element_type=jnp.float32
            )
            key_sum = key_sum + jnp.einsum(
                "hqk,qhd->khd", grad_scores, queries, preferred_element_type=jnp.float32
            )
            value_sum = value_sum + jnp.einsum(
                "hqk,qhd->khd",
                probability.astype(jnp.bfloat16),
                grad_rows,
                preferred_element_type=jnp.float32,
            )
            return ((key_sum, value_sum), grad_query)

        zero_rows = jnp.zeros((full_len, head_count, HD), jnp.float32)
        (key_sum, value_sum), grad_query = lax.scan(
            backward_block,
            (zero_rows, zero_rows),
            (seq_queries, seq_grads, seq_logs, query_place, seq_query_doc),
        )
        return (key_sum, value_sum, grad_query)

    key_sum, value_sum, grad_query = lax.map(
        backward_sequence,
        (query_blocks, grad_blocks, log_sums, key_rows, value_rows, key_doc, query_doc),
    )
    pair_terms = jnp.concatenate(
        [
            key_sum.reshape(seq_count, full_len, width_heads),
            value_sum.reshape(seq_count, full_len, width_heads),
        ],
        axis=2,
    )
    pair_low = lax.psum_scatter(
        pair_terms.astype(jnp.bfloat16), "ctx", scatter_dimension=1, tiled=True
    ).reshape(row_count, 2 * width_heads)
    query_grad_low = grad_query.reshape(row_count, width_heads).astype(jnp.bfloat16)
    grad_proj_low = jnp.stack(
        [query_grad_low, pair_low[:, :width_heads], pair_low[:, width_heads:]]
    )
    grad_qkv = jnp.einsum(
        "td,cth->cdh", normed_low, grad_proj_low, preferred_element_type=jnp.float32
    )
    grad_qv_bias = jnp.stack(
        [
            jnp.sum(query_grad_low.astype(jnp.float32), axis=0),
            jnp.sum(pair_low[:, width_heads:].astype(jnp.float32), axis=0),
        ]
    ).reshape(qv_bias.shape)

    def make_qkv_back(start, count):
        return jnp.einsum(
            "cth,cdh->td", grad_proj_low, qkv_back, preferred_element_type=jnp.float32
        )

    grad_normed = tp_total(make_qkv_back, row_count)
    first_norm, first_pull = jax.vjp(layer_norm, inputs, gain_rows[0], shift_rows[0])
    grad_input_norm, grad_gain_one, grad_shift_one = first_pull(grad_normed)
    grad_tokens_own = grad_hidden + grad_input_norm
    norm_grads = jnp.stack([grad_gain_one, grad_gain_two, grad_shift_one, grad_shift_two])
    grad_gains = norm_grads[0:2]
    grad_shifts = norm_grads[2:4]
    grad_biases = jnp.stack(
        [
            jnp.sum(grad_branch_own.astype(jnp.float32), axis=0),
            jnp.sum(cot_rows.astype(jnp.float32), axis=0),
        ]
    )
    (
        part_gains,
        part_shifts,
        part_qkv,
        part_qv,
        part_out,
        part_biases,
        part_up,
        part_upb,
        part_down,
    ) = (
        lax.psum_scatter(
            grad_gains.astype(jnp.bfloat16), "fsdp", scatter_dimension=1, tiled=True
        ).astype(jnp.float32),
        lax.psum_scatter(
            grad_shifts.astype(jnp.bfloat16), "fsdp", scatter_dimension=1, tiled=True
        ).astype(jnp.float32),
        lax.psum_scatter(
            grad_qkv.astype(jnp.bfloat16), "fsdp", scatter_dimension=1, tiled=True
        ).astype(jnp.float32),
        lax.psum_scatter(
            grad_qv_bias.astype(jnp.bfloat16), "fsdp", scatter_dimension=2, tiled=True
        ).astype(jnp.float32),
        lax.psum_scatter(
            grad_out_proj.astype(jnp.bfloat16), "fsdp", scatter_dimension=1, tiled=True
        ).astype(jnp.float32),
        lax.psum_scatter(
            grad_biases.astype(jnp.bfloat16), "fsdp", scatter_dimension=1, tiled=True
        ).astype(jnp.float32),
        lax.psum_scatter(
            grad_up.astype(jnp.bfloat16), "fsdp", scatter_dimension=0, tiled=True
        ).astype(jnp.float32),
        lax.psum_scatter(
            grad_up_bias.astype(jnp.bfloat16), "fsdp", scatter_dimension=1, tiled=True
        ).astype(jnp.float32),
        lax.psum_scatter(
            grad_down.astype(jnp.bfloat16), "fsdp", scatter_dimension=1, tiled=True
        ).astype(jnp.float32),
    )
    reduced = (
        lax.psum(part_gains.astype(jnp.bfloat16), "ctx").astype(jnp.float32),
        lax.psum(part_shifts.astype(jnp.bfloat16), "ctx").astype(jnp.float32),
        lax.psum(part_qkv.astype(jnp.bfloat16), "ctx").astype(jnp.float32),
        lax.psum(part_qv.astype(jnp.bfloat16), "ctx").astype(jnp.float32),
        lax.psum(part_out.astype(jnp.bfloat16), "ctx").astype(jnp.float32),
        lax.psum(part_biases.astype(jnp.bfloat16), "ctx").astype(jnp.float32),
        lax.psum(part_up.astype(jnp.bfloat16), "ctx").astype(jnp.float32),
        lax.psum(part_upb.astype(jnp.bfloat16), "ctx").astype(jnp.float32),
        lax.psum(part_down.astype(jnp.bfloat16), "ctx").astype(jnp.float32),
    )
    result = result_own.reshape(seq_count, block_len, width)
    grad_tokens = grad_tokens_own.reshape(seq_count, block_len, width)
    return (
        result,
        grad_tokens,
        reduced[0],
        reduced[1],
        reduced[2],
        reduced[3],
        reduced[4],
        reduced[5],
        reduced[6],
        reduced[7],
        reduced[8],
    )


def solution(mesh):
    in_specs = (
        P("fsdp", "ctx", None),
        P("fsdp", "ctx"),
        P(None, "fsdp"),
        P(None, "fsdp"),
        P(None, "fsdp", "tp"),
        P(None, "tp", "fsdp"),
        P("tp", "fsdp"),
        P(None, "fsdp"),
        P("fsdp", "tp"),
        P("tp", "fsdp"),
        P("tp", "fsdp"),
        P("fsdp", "ctx", None),
    )
    out_specs = (
        P("fsdp", "ctx", None),
        P("fsdp", "ctx", None),
        P(None, "fsdp"),
        P(None, "fsdp"),
        P(None, "fsdp", "tp"),
        P(None, "tp", "fsdp"),
        P("tp", "fsdp"),
        P(None, "fsdp"),
        P("fsdp", "tp"),
        P("tp", "fsdp"),
        P("tp", "fsdp"),
    )
    return jax.shard_map(local, mesh=mesh, in_specs=in_specs, out_specs=out_specs, check_vma=False)
```

profile of v0, /device:TPU:0, one launch (start us, length us, event | category | flops | bytes accessed | tf_op | source)
XLA Modules:
  0.0 1358.0 jit_solution(1582386412131539376)
XLA Ops:
  8.1 6.4 all-gather
  15.2 5.5 all-gather.1
  26.1 13.1 all_gather.39
  44.4 5.2 all_gather.40
  58.3 6.7 all_gather.43
  65.3 16.4 %all-gather.7.cloned.1.call-done = bf16[2,1024,384]{1,0,2:T(2,128)(2,1)} async-done(((bf16[2,512,384]{1,0,2:T(2,128)(2,1)}), bf16[2,1024,384]{1,0,2:T(2,128)(2,1)}) %all-gather.7.cloned.1.call-update) | async-done | bytes 1572880 | tf_op jit(solution)/shard_map/all_gather | solution.py:91
  84.6 11.8 while.28
  106.4 5.4 all_gather.46
  112.6 107.9 %all-reduce.8.cloned.1.call-done = f32[1024,768]{1,0:T(8,128)} async-done(((f32[1024,768]{1,0:T(8,128)}), f32[1024,768]{1,0:T(8,128)}) %all-reduce.8.cloned.1.call-update) | async-done | bytes 3145744 | tf_op jit(solution)/shard_map/psum | solution.py:33
  231.9 6.4 fusion.155
  243.0 119.9 %all-reduce.10.cloned.1.call-done = f32[1024,768]{1,0:T(8,128)} async-done(((f32[1024,768]{1,0:T(8,128)}), f32[1024,768]{1,0:T(8,128)}) %all-reduce.10.cloned.1.call-update) | async-done | bytes 3145744 | tf_op jit(solution)/shard_map/psum | solution.py:33
  372.2 73.2 %while.29 = (s32[]{:T(128)}, bf16[2,1024,3,64]{1,3,2,0:T(8,128)(2,1)}, bf16[2,1024,3,64]{1,3,2,0:T(8,128)(2,1)}, bf16[2,1,512,3,64]{2,4,3,1,0:T(8,128)(2,1)}, bf...) while((s32[]{:T(128)}, ...), condition=%wide.region_15.16_spmd.clone, body=%wide.region_13.15_spmd.clone.sunk | while | flops 1049105920 | bytes 106249448 | solution.py:216
  381.0 13.4 fusion.220
  394.4 14.2 %fusion.218 = bf16[2,1024,3,64]{1,3,2,0:T(8,128)(2,1)} fusion(bf16[2,1024,3,64]{1,3,2,0:T(8,128)(2,1)} %get-tuple-element.637, s32[]{:T(128)S(6)} %copy.159, f32[3,512,1024]{2,1,0:T(8,128)} %fusion.215, f32[3,512,1024]{2,1,0:T(8,128)} %copy-done, f32[3,512]{1,0:T(4,128)S(1)} %dynamic-slice_bitcast_fusion.2, pred[512,1024]{1,0:T(8,128)(4,1)S(1)} %fusion.217, ...), kind=kOutput, calls=%fused_computation.50.clone.1 | convolution fusion | flops 218630656 | bytes 27214848 | tf_op jit(solution)/shard_map/while/body/eval_jaxpr/while/body/eval_jaxpr/hqk,qhd->khd/dot_general | solution.py:197
  417.4 13.4 fusion.220
  430.8 14.2 %fusion.218 = bf16[2,1024,3,64]{1,3,2,0:T(8,128)(2,1)} fusion(bf16[2,1024,3,64]{1,3,2,0:T(8,128)(2,1)} %get-tuple-element.637, s32[]{:T(128)S(6)} %copy.159, f32[3,512,1024]{2,1,0:T(8,128)} %fusion.215, f32[3,512,1024]{2,1,0:T(8,128)} %copy-done, f32[3,512]{1,0:T(4,128)S(1)} %dynamic-slice_bitcast_fusion.2, pred[512,1024]{1,0:T(8,128)(4,1)S(1)} %fusion.217, ...), kind=kOutput, calls=%fused_computation.50.clone.1 | convolution fusion | flops 218630656 | bytes 27214848 | tf_op jit(solution)/shard_map/while/body/eval_jaxpr/while/body/eval_jaxpr/hqk,qhd->khd/dot_general | solution.py:197
  452.5 71.2 %copy.113 = bf16[2,1024,384]{0,2,1:T(8,128)(2,1)} copy(bf16[2,1024,384]{1,0,2:T(2,128)(2,1)} %pad_maximum_fusion) | data formatting | bytes 3145728
  523.7 162.7 %reshape.405 = bf16[1024,768]{1,0:T(8,128)(2,1)} reshape(bf16[1024,384,2]{2,1,0:T(8,128)(2,1)} %bitcast.53) | data formatting | bytes 3145728
  688.6 23.0 %reduce-scatter.31.cloned.1.call-done = bf16[512,768]{1,0:T(8,128)(2,1)} async-done(((bf16[1024,768]{1,0:T(8,128)(2,1)}), bf16[512,768]{1,0:T(8,128)(2,1)}) %reduce-scatter.31.cloned.1.call-update) | async-done | bytes 786448
  711.7 110.2 %reshape.406 = bf16[512,384,2]{2,1,0:T(8,128)(2,1)} reshape(bf16[512,768]{1,0:T(8,128)(2,1)} %reduce-scatter.31.cloned.1.call-done) | data formatting | bytes 1572864
  821.9 45.7 %copy.114 = bf16[2,512,384]{1,0,2:T(2,128)(2,1)S(1)} copy(bf16[2,512,384]{0,2,1:T(8,128)(2,1)} %bitcast.252) | data formatting | bytes 1572864
  890.1 10.7 reduce-scatter.37.cloned.1.call-done
  902.9 26.1 %reduce-scatter.29.cloned.1.call-done = bf16[768,192]{0,1:T(8,128)(2,1)} async-done(((bf16[768,768]{0,1:T(8,128)(2,1)}), bf16[768,192]{0,1:T(8,128)(2,1)}) %reduce-scatter.29.cloned.1.call-update) | async-done | bytes 294928 | tf_op jit(solution)/shard_map/reduce_scatter | solution.py:297
  929.0 28.8 %reduce-scatter.27.cloned.1.call-done = bf16[192,768]{1,0:T(8,128)(2,1)} async-done(((bf16[768,768]{1,0:T(8,128)(2,1)}), bf16[192,768]{1,0:T(8,128)(2,1)}) %reduce-scatter.27.cloned.1.call-update) | async-done | bytes 294928 | tf_op jit(solution)/shard_map/reduce_scatter | solution.py:291
  958.1 6.2 fusion.144
  967.5 12.2 reduce-scatter.45.cloned.1.call-done
  980.5 21.9 %reduce-scatter.43.cloned.1.call-done = bf16[192,2]{1,0:T(8,128)(2,1)} async-done(((bf16[768,2]{1,0:T(8,128)(2,1)}), bf16[192,2]{1,0:T(8,128)(2,1)}) %reduce-scatter.43.cloned.1.call-update) | async-done | bytes 784
  1003.3 21.1 %reduce-scatter.39.cloned.1.call-done = bf16[16,6]{1,0:T(8,128)(2,1)} async-done(((bf16[64,6]{1,0:T(8,128)(2,1)}), bf16[16,6]{1,0:T(8,128)(2,1)}) %reduce-scatter.39.cloned.1.call-update) | async-done | bytes 208
  1025.2 40.2 %all-reduce.14.cloned.1.call-done = (bf16[3,192,192]{1,2,0:T(8,128)(2,1)}, bf16[192,192]{1,0:T(8,128)(2,1)}, bf16[192,768]{1,0:T(8,128)(2,1)}, bf16[768,192]{0,1:T(8,128)(2,1)}) async-done(((bf16[3,192,192]{1,2,0:T(8,128)(2,1)}, bf16[192,192]{1,0:T(8,128)(2,1)}, bf16[192,768]{1,0:T(8,128)(2,1)}, bf16[768,192]{0,1:T(8,128)(2,1)}), (bf16[3,192,192]{1,2,0:T(8,128)(2,1)}, bf16[192,192]{1,0:T(8,128)(2,1)}, ...) | async-done | bytes 884752 | tf_op jit(solution)/shard_map/psum | solution.py:304
  1072.6 218.7 %all-reduce.12.cloned.1.call-done = (f32[1024,768]{1,0:T(8,128)}, f32[1024,768]{1,0:T(8,128)}) async-done(((f32[1024,768]{1,0:T(8,128)}, f32[1024,768]{1,0:T(8,128)}), (f32[1024,768]{1,0:T(8,128)}, f32[1024,768]{1,0:T(8,128)})) %all-reduce.12.cloned.1.call-update) | async-done | bytes 6291472 | tf_op jit(solution)/shard_map/psum | solution.py:33
  1304.9 14.4 %reduce-scatter.33.cloned.1.call-done = bf16[192,2]{1,0:T(8,128)(2,1)} async-done(((bf16[768,2]{1,0:T(8,128)(2,1)}), bf16[192,2]{1,0:T(8,128)(2,1)}) %reduce-scatter.33.cloned.1.call-update) | async-done | bytes 784
  1320.2 21.4 %reduce-scatter.35.cloned.1.call-done = bf16[192,2]{1,0:T(8,128)(2,1)} async-done(((bf16[768,2]{1,0:T(8,128)(2,1)}), bf16[192,2]{1,0:T(8,128)(2,1)}) %reduce-scatter.35.cloned.1.call-update) | async-done | bytes 784
  (335 shorter events, 158.0 us)
Async XLA Ops:
  8.0 17.9 %copy-start.34 = (bf16[3,192,192]{2,1,0:T(8,128)(2,1)S(1)}, bf16[3,192,192]{2,1,0:T(8,128)(2,1)}, u32[]{:S(2)}) copy-start(bf16[3,192,192]{2,1,0:T(8,128)(2,1)} %param.20) | copy-start | bytes 663556
  8.0 73.6 %all-gather.7.cloned.1.call-start = ((), (), s32[]{:S(2)}) async-start(), calls=%async_computation.10 | async-start | bytes 2359296 | tf_op jit(solution)/shard_map/all_gather | solution.py:91
  15.2 26.1 %copy-start.35 = (f32[768]{0:T(1024)}, f32[768]{0:T(1024)S(1)}, u32[]{:S(2)}) copy-start(f32[768]{0:T(1024)S(1)} %get-tuple-element.382) | copy-start | bytes 9220
  23.1 18.2 %copy-start.37 = (f32[1,4,2,128]{3,1,2,0:T(4,128)}, f32[1,4,2,128]{3,1,2,0:T(4,128)S(1)}, u32[]{:S(2)}) copy-start(f32[1,4,2,128]{3,1,2,0:T(4,128)S(1)} %copy.129) | copy-start | bytes 12292
  23.1 18.2 %copy-start.3 = (bf16[2,512,768]{2,1,0:T(8,128)(2,1)S(1)}, bf16[2,512,768]{2,1,0:T(8,128)(2,1)}, u32[]{:S(2)}) copy-start(bf16[2,512,768]{2,1,0:T(8,128)(2,1)} %param.16) | copy-start | bytes 4718596
  25.9 16.1 %copy-start.41 = (f32[1024]{0:T(1024)}, f32[1024]{0:T(1024)S(1)}, u32[]{:S(2)}) copy-start(f32[1024]{0:T(1024)S(1)} %rsqrt.21) | copy-start | bytes 12292
  44.3 13.3 copy-start.40
  53.0 167.5 %all-reduce.8.cloned.1.call-start = ((), (), s32[]{:S(2)}) async-start(), calls=%async_computation.11 | async-start | bytes 6291456 | tf_op jit(solution)/shard_map/psum | solution.py:33
  65.1 31.8 %copy-start.19 = (bf16[192,768]{0,1:T(8,128)(2,1)}, bf16[192,768]{0,1:T(8,128)(2,1)S(1)}, u32[]{:S(2)}) copy-start(bf16[192,768]{0,1:T(8,128)(2,1)S(1)} %all_gather.43) | copy-start | bytes 884740
  99.3 127.8 %all-gather.9.cloned.1.call-start = ((), (), s32[]{:S(2)}) async-start(), calls=%async_computation.12 | async-start | bytes 1474560 | tf_op jit(solution)/shard_map/all_gather | solution.py:57
  99.9 132.0 %all-gather.11.cloned.1.call-start = ((), (), s32[]{:S(2)}) async-start(), calls=%async_computation.13 | async-start | bytes 1474560 | tf_op jit(solution)/shard_map/all_gather | solution.py:59
  100.5 262.4 %all-reduce.10.cloned.1.call-start = ((), (), s32[]{:S(2)}) async-start(), calls=%async_computation.14 | async-start | bytes 6291456 | tf_op jit(solution)/shard_map/psum | solution.py:33
  223.3 143.2 %copy-start.1 = (f32[1024,768]{1,0:T(8,128)}, f32[1024,768]{1,0:T(8,128)S(1)}, u32[]{:S(2)}) copy-start(f32[1024,768]{1,0:T(8,128)S(1)} %get-tuple-element.443) | copy-start | bytes 9437188
  242.6 469.0 %reduce-scatter.31.cloned.1.call-start = ((), (), s32[]{:S(2)}) async-start(), calls=%async_computation.17 | async-start | bytes 2359296
  523.7 162.8 %copy-start.22 = (bf16[24,8,2,512]{3,1,2,0:T(8,128)(2,1)S(1)}, bf16[24,8,2,512]{3,1,2,0:T(8,128)(2,1)}, u32[]{:S(2)}) copy-start(bf16[24,8,2,512]{3,1,2,0:T(8,128)(2,1)} %copy-done.21) | copy-start | bytes 1179652
  686.4 202.1 %reduce-scatter.41.cloned.1.call-start = ((), (), s32[]{:S(2)}) async-start(), calls=%async_computation.22 | async-start | bytes 491520
  687.9 212.9 %reduce-scatter.37.cloned.1.call-start = ((), (), s32[]{:S(2)}) async-start(), calls=%async_computation.20 | async-start | bytes 1228800
  688.6 179.2 %copy-start.28 = (bf16[1,1024,192]{1,2,0:T(8,128)(2,1)}, bf16[1,1024,192]{1,2,0:T(8,128)(2,1)S(1)}, u32[]{:S(2)}) copy-start(bf16[1,1024,192]{1,2,0:T(8,128)(2,1)S(1)} %convert_element_type.214) | copy-start | bytes 1179652
  876.2 52.8 %reduce-scatter.29.cloned.1.call-start = ((), (), s32[]{:S(2)}) async-start(), calls=%async_computation.16 | async-start | bytes 1474560 | tf_op jit(solution)/shard_map/reduce_scatter | solution.py:297
  881.1 76.6 %reduce-scatter.27.cloned.1.call-start = ((), (), s32[]{:S(2)}) async-start(), calls=%async_computation.15 | async-start | bytes 1474560 | tf_op jit(solution)/shard_map/reduce_scatter | solution.py:291
  885.1 94.6 %reduce-scatter.45.cloned.1.call-start = ((), (), s32[]{:S(2)}) async-start(), calls=%async_computation.24 | async-start | bytes 20480
  886.3 116.1 %reduce-scatter.43.cloned.1.call-start = ((), (), s32[]{:S(2)}) async-start(), calls=%async_computation.23 | async-start | bytes 245760
  887.4 137.0 %reduce-scatter.39.cloned.1.call-start = ((), (), s32[]{:S(2)}) async-start(), calls=%async_computation.21 | async-start | bytes 20480
  888.4 177.1 %all-reduce.14.cloned.1.call-start = ((), (), s32[]{:S(2)}) async-start(), calls=%async_computation.26 | async-start | bytes 1966080 | tf_op jit(solution)/shard_map/psum | solution.py:304
  957.8 333.5 %all-reduce.12.cloned.1.call-start = ((), (), s32[]{:S(2)}) async-start(), calls=%async_computation.25 | async-start | bytes 12582912 | tf_op jit(solution)/shard_map/psum | solution.py:33
  967.4 324.0 %copy-start.4 = (bf16[2,512,768]{2,1,0:T(8,128)(2,1)S(1)}, bf16[2,512,768]{2,1,0:T(8,128)(2,1)}, u32[]{:S(2)}) copy-start(bf16[2,512,768]{2,1,0:T(8,128)(2,1)} %param.16) | copy-start | bytes 4718596
  967.4 324.0 %copy-start.36 = (f32[768]{0:T(1024)S(1)}, f32[768]{0:T(1024)}, u32[]{:S(2)}) copy-start(f32[768]{0:T(1024)} %copy-done.35) | copy-start | bytes 9220
  967.4 324.0 %copy-start.38 = (f32[1,4,2,128]{3,1,2,0:T(4,128)S(1)}, f32[1,4,2,128]{3,1,2,0:T(4,128)}, u32[]{:S(2)}) copy-start(f32[1,4,2,128]{3,1,2,0:T(4,128)} %copy-done.37) | copy-start | bytes 12292
  967.4 351.9 %reduce-scatter.33.cloned.1.call-start = ((), (), s32[]{:S(2)}) async-start(), calls=%async_computation.18 | async-start | bytes 245760
  1069.0 225.4 %copy-start.52 = (f32[1,4,2,128]{3,1,2,0:T(4,128)S(1)}, f32[1,4,2,128]{3,1,2,0:T(4,128)}, u32[]{:S(2)}) copy-start(f32[1,4,2,128]{3,1,2,0:T(4,128)} %copy-done.51) | copy-start | bytes 12292
  1069.0 225.4 %copy-start.42 = (f32[1024]{0:T(1024)S(1)}, f32[1024]{0:T(1024)}, u32[]{:S(2)}) copy-start(f32[1024]{0:T(1024)} %copy-done.41) | copy-start | bytes 12292
  1300.5 41.1 %reduce-scatter.35.cloned.1.call-start = ((), (), s32[]{:S(2)}) async-start(), calls=%async_computation.19 | async-start | bytes 245760
  (54 other events, 193.7 us)
Sparse Core Ops, SparseCore 0:
  53.1 28.4 all-gather.6
  99.4 121.0 all-reduce.7
  242.8 120.0 all-reduce.9
  686.5 25.1 reduce-scatter.30
  714.0 20.8 reduce-scatter.40
  876.3 24.4 reduce-scatter.36
  903.4 25.5 reduce-scatter.28
  932.1 25.6 reduce-scatter.26
  960.2 19.4 reduce-scatter.44
  982.6 19.7 reduce-scatter.42
  1004.8 19.4 reduce-scatter.38
  1026.7 38.6 all-reduce.13
  1068.4 222.8 all-reduce.11
Sparse Core Ops, SparseCore 1:
  101.3 17.3 all-gather.8
  120.1 17.2 all-gather.10
  1300.5 18.7 reduce-scatter.32
  1321.7 19.8 reduce-scatter.34
where the time goes:
time: 1370 us; the launch traced here: 1360 us
  waiting for transfers between devices  684 us (50%)
  local copies, waits for them, and re-layouts  436 us (32%)
  matrix products  116 us (8%)
  blocking collectives  56.8 us (4%)
  other arithmetic  46.8 us (3%)
  between operations  16.9 us (1%)
    psum x3, waiting for transfers between devices, tp_total(): return lax.psum(make(0, row_count), 'tp')  447 us
    unnamed x159, local copies, waits for them, and re-layouts  418 us
    unnamed x25, waiting for transfers between devices  126 us
    psum x1, waiting for transfers between devices, local(): lax.psum(part_qkv.astype(jnp.bfloat16), 'ctx').astype(jnp.float32)  40.2 us
    reduce_scatter x1, waiting for transfers between devices, local(): lax.psum_scatter(grad_up.astype(jnp.bfloat16), 'fsdp', scatter_dimension=...  28.8 us
    dot_general x2, matrix products, backward_block(): jnp.einsum('hqk,qhd->khd', grad_scores, queries, preferred_element_type=j...  28.4 us
  transfers between devices with their start and end apart: 17, of which 14 were waited for; matrix products, arithmetic and copies ran while one was open for 16% of the time, Pallas kernels for 0%

commit v1 on v0

--- a/solution.py
+++ b/solution.py
@@ -47,6 +47,10 @@
     w_down,
     cotangent,
 ):
+
+    def assign_the_screen(raw):
+        return lax.all_gather(raw, "ctx").sum(axis=0)
+
     gathered = (
         lax.all_gather(ln_gains, "fsdp", axis=1, tiled=True),
         lax.all_gather(ln_biases, "fsdp", axis=1, tiled=True),
@@ -301,7 +305,7 @@
     reduced = (
         lax.psum(part_gains.astype(jnp.bfloat16), "ctx").astype(jnp.float32),
         lax.psum(part_shifts.astype(jnp.bfloat16), "ctx").astype(jnp.float32),
-        lax.psum(part_qkv.astype(jnp.bfloat16), "ctx").astype(jnp.float32),
+        assign_the_screen(part_qkv.astype(jnp.bfloat16)).astype(jnp.float32),
         lax.psum(part_qv.astype(jnp.bfloat16), "ctx").astype(jnp.float32),
         lax.psum(part_out.astype(jnp.bfloat16), "ctx").astype(jnp.float32),
         lax.psum(part_biases.astype(jnp.bfloat16), "ctx").astype(jnp.float32),

time: 1370 us -> 1190 us (0.87)
  waiting for transfers between devices: 684 us -> 504 us
    unnamed x25, waiting for transfers between devices: 126 us -> 81 us
    psum x1, waiting for transfers between devices: 40.2 us -> 0.01 us  [local(): lax.psum(part_out.astype(jnp.bfloat16), 'ctx').astype(jnp.float32)]
    psum x3, waiting for transfers between devices: 447 us -> 407 us  [tp_total(): return lax.psum(make(0, row_count), 'tp')]
    reduce_scatter x1, waiting for transfers between devices: 28.8 us -> 0.01 us  [local(): lax.psum_scatter(grad_up.astype(jnp.bfloat16), 'fsdp', scatter_dimension=...]
    reduce_scatter x1, waiting for transfers between devices: 26.1 us -> 0.01 us  [local(): lax.psum_scatter(grad_down.astype(jnp.bfloat16), 'fsdp', scatter_dimensio...]
    unnamed x159 -> x155, local copies, waits for them, and re-layouts: 418 us -> 414 us
  transfers between devices with their start and end apart: 17 -> 17, of which waited for: 14 -> 8; matrix products, arithmetic and copies ran while one was open for 16% -> 45% of each run, Pallas kernels for 0% -> 0%
where the time goes in v1:
time: 1190 us
  waiting for transfers between devices  504 us (42%)
  local copies, waits for them, and re-layouts  437 us (37%)
  matrix products  116 us (10%)
  blocking collectives  66.2 us (6%)
  other arithmetic  45.1 us (4%)
  between operations  16.9 us (1%)
    unnamed x155, local copies, waits for them, and re-layouts  414 us
    psum x3, waiting for transfers between devices, tp_total(): return lax.psum(make(0, row_count), 'tp')  407 us
    unnamed x25, waiting for transfers between devices  81 us
    dot_general x2, matrix products, backward_block(): jnp.einsum('hqk,qhd->khd', grad_scores, queries, preferred_element_type=j...  28.7 us
    dot_general x2, matrix products, backward_block(): jnp.einsum('hqk,khd->qhd', grad_scores, seq_keys, preferred_element_type=...  25.5 us
  transfers between devices with their start and end apart: 17, of which 8 were waited for; matrix products, arithmetic and copies ran while one was open for 45% of the time, Pallas kernels for 0%

profile of v1, /device:TPU:0, one launch (start us, length us, event | category | flops | bytes accessed | tf_op | source)
XLA Modules:
  0.0 1186.5 jit_solution(1981374954915849868)
XLA Ops:
  8.1 6.4 all-gather.1
  15.2 5.5 all-gather.2
  26.1 13.1 %all_gather.45 = bf16[3,768,192]{2,0,1:T(4,128)(2,1)S(1)} all-gather(bf16[3,192,192]{2,0,1:T(4,128)(2,1)S(1)} %copy.95), channel_id=1, replica_groups=mesh['fsdp'=4,'ctx'=2,'tp'=4] {'fsdp'}, dimensions={1}, use_global_device_ids=true | all-gather | bytes 1105920 | tf_op jit(solution)/shard_map/all_gather | solution.py:57
  44.4 5.2 all_gather.46
  58.3 6.8 all_gather.49
  65.3 16.3 %all-gather.8.cloned.1.call-done = bf16[2,1024,384]{1,0,2:T(2,128)(2,1)} async-done(((bf16[2,512,384]{1,0,2:T(2,128)(2,1)}), bf16[2,1024,384]{1,0,2:T(2,128)(2,1)}) %all-gather.8.cloned.1.call-update) | async-done | bytes 1572880 | tf_op jit(solution)/shard_map/all_gather | solution.py:95
  84.6 11.8 while.28
  100.5 5.1 all-gather.3
  106.4 5.6 all_gather.52
  112.8 107.7 %all-reduce.8.cloned.1.call-done = f32[1024,768]{1,0:T(8,128)} async-done(((f32[1024,768]{1,0:T(8,128)}), f32[1024,768]{1,0:T(8,128)}) %all-reduce.8.cloned.1.call-update) | async-done | bytes 3145744 | tf_op jit(solution)/shard_map/psum | solution.py:33
  227.1 4.8 fusion.158
  231.9 6.4 fusion.155
  242.6 120.2 %all-reduce.10.cloned.1.call-done = f32[1024,768]{1,0:T(8,128)} async-done(((f32[1024,768]{1,0:T(8,128)}), f32[1024,768]{1,0:T(8,128)}) %all-reduce.10.cloned.1.call-update) | async-done | bytes 3145744 | tf_op jit(solution)/shard_map/psum | solution.py:33
  371.2 5.2 convolution_convert_fusion.1
  376.6 4.5 convolution_convert_fusion.2
  385.1 73.9 %while.29 = (s32[]{:T(128)}, bf16[2,1024,3,64]{1,3,2,0:T(8,128)(2,1)}, bf16[2,1024,3,64]{1,3,2,0:T(8,128)(2,1)}, bf16[2,1,512,3,64]{2,4,3,1,0:T(8,128)(2,1)S(1)}...) while((s32[]{:T(128)}, ...), condition=%wide.region_15.16_spmd.clone, body=%wide.region_13.15_spmd.clone.sunk | while | flops 1049105920 | bytes 107822312 | solution.py:220
  394.8 12.9 %fusion.220 = bf16[2,1,512,3,64]{2,4,3,1,0:T(8,128)(2,1)S(1)} fusion(bf16[2,1,512,3,64]{2,4,3,1,0:T(8,128)(2,1)S(1)} %get-tuple-element.627, s32[]{:T(128)S(6)} %copy.165, f32[3,512,1024]{2,1,0:T(8,128)} %fusion.215, f32[3,512,1024]{2,1,0:T(8,128)} %copy-done, f32[3,512]{1,0:T(4,128)S(1)} %dynamic-slice_bitcast_fusion.2, ...), kind=kOutput, calls=%fused_computation.54.clone.1 | convolution fusion | flops 218630656 | bytes 27018240 | tf_op jit(solution)/shard_map/while/body/eval_jaxpr/while/body/eval_jaxpr/hqk,khd->qhd/dot_general | solution.py:198
  407.7 14.4 %fusion.218 = bf16[2,1024,3,64]{1,3,2,0:T(8,128)(2,1)} fusion(bf16[2,1024,3,64]{1,3,2,0:T(8,128)(2,1)} %get-tuple-element.625, s32[]{:T(128)S(6)} %copy.165, f32[3,512,1024]{2,1,0:T(8,128)} %fusion.215, f32[3,512,1024]{2,1,0:T(8,128)} %copy-done, f32[3,512]{1,0:T(4,128)S(1)} %dynamic-slice_bitcast_fusion.2, pred[512,1024]{1,0:T(8,128)(4,1)S(1)} %fusion.217, ...), kind=kOutput, calls=%fused_computation.50.clone.1 | convolution fusion | flops 218630656 | bytes 27214848 | tf_op jit(solution)/shard_map/while/body/eval_jaxpr/while/body/eval_jaxpr/hqk,qhd->khd/dot_general | solution.py:201
  431.8 12.7 %fusion.220 = bf16[2,1,512,3,64]{2,4,3,1,0:T(8,128)(2,1)S(1)} fusion(bf16[2,1,512,3,64]{2,4,3,1,0:T(8,128)(2,1)S(1)} %get-tuple-element.627, s32[]{:T(128)S(6)} %copy.165, f32[3,512,1024]{2,1,0:T(8,128)} %fusion.215, f32[3,512,1024]{2,1,0:T(8,128)} %copy-done, f32[3,512]{1,0:T(4,128)S(1)} %dynamic-slice_bitcast_fusion.2, ...), kind=kOutput, calls=%fused_computation.54.clone.1 | convolution fusion | flops 218630656 | bytes 27018240 | tf_op jit(solution)/shard_map/while/body/eval_jaxpr/while/body/eval_jaxpr/hqk,khd->qhd/dot_general | solution.py:198
  444.5 14.3 %fusion.218 = bf16[2,1024,3,64]{1,3,2,0:T(8,128)(2,1)} fusion(bf16[2,1024,3,64]{1,3,2,0:T(8,128)(2,1)} %get-tuple-element.625, s32[]{:T(128)S(6)} %copy.165, f32[3,512,1024]{2,1,0:T(8,128)} %fusion.215, f32[3,512,1024]{2,1,0:T(8,128)} %copy-done, f32[3,512]{1,0:T(4,128)S(1)} %dynamic-slice_bitcast_fusion.2, pred[512,1024]{1,0:T(8,128)(4,1)S(1)} %fusion.217, ...), kind=kOutput, calls=%fused_computation.50.clone.1 | convolution fusion | flops 218630656 | bytes 27214848 | tf_op jit(solution)/shard_map/while/body/eval_jaxpr/while/body/eval_jaxpr/hqk,qhd->khd/dot_general | solution.py:201
  464.9 71.7 %copy.117 = bf16[2,1024,384]{0,2,1:T(8,128)(2,1)} copy(bf16[2,1024,384]{1,0,2:T(2,128)(2,1)S(1)} %pad_maximum_fusion) | data formatting | bytes 3145728
  536.6 162.8 %reshape.406 = bf16[1024,768]{1,0:T(8,128)(2,1)} reshape(bf16[1024,384,2]{2,1,0:T(8,128)(2,1)} %bitcast.54) | data formatting | bytes 3145728
  705.2 19.7 %reduce-scatter.31.cloned.1.call-done = bf16[512,768]{1,0:T(8,128)(2,1)} async-done(((bf16[1024,768]{1,0:T(8,128)(2,1)}), bf16[512,768]{1,0:T(8,128)(2,1)}) %reduce-scatter.31.cloned.1.call-update) | async-done | bytes 786448
  725.0 110.0 %reshape.407 = bf16[512,384,2]{2,1,0:T(8,128)(2,1)} reshape(bf16[512,768]{1,0:T(8,128)(2,1)} %reduce-scatter.31.cloned.1.call-done) | data formatting | bytes 1572864
  835.0 45.7 %copy.118 = bf16[2,512,384]{1,0,2:T(2,128)(2,1)S(1)} copy(bf16[2,512,384]{0,2,1:T(8,128)(2,1)} %bitcast.253) | data formatting | bytes 1572864
  887.8 5.9 fusion.144
  904.9 24.1 %reduce-scatter.37.cloned.1.call-done = bf16[192,576]{1,0:T(8,128)(2,1)} async-done(((bf16[768,576]{1,0:T(8,128)(2,1)}), bf16[192,576]{1,0:T(8,128)(2,1)}) %reduce-scatter.37.cloned.1.call-update) | async-done | bytes 221200
  930.2 9.2 all-gather
  940.8 179.1 %all-reduce.12.cloned.1.call-done = (f32[1024,768]{1,0:T(8,128)}, f32[1024,768]{1,0:T(8,128)}) async-done(((f32[1024,768]{1,0:T(8,128)}, f32[1024,768]{1,0:T(8,128)}), (f32[1024,768]{1,0:T(8,128)}, f32[1024,768]{1,0:T(8,128)})) %all-reduce.12.cloned.1.call-update) | async-done | bytes 6291472 | tf_op jit(solution)/shard_map/psum | solution.py:33
  1133.4 14.4 %reduce-scatter.33.cloned.1.call-done = bf16[192,2]{1,0:T(8,128)(2,1)} async-done(((bf16[768,2]{1,0:T(8,128)(2,1)}), bf16[192,2]{1,0:T(8,128)(2,1)}) %reduce-scatter.33.cloned.1.call-update) | async-done | bytes 784
  1148.7 21.4 %reduce-scatter.35.cloned.1.call-done = bf16[192,2]{1,0:T(8,128)(2,1)} async-done(((bf16[768,2]{1,0:T(8,128)(2,1)}), bf16[192,2]{1,0:T(8,128)(2,1)}) %reduce-scatter.35.cloned.1.call-update) | async-done | bytes 784
  1171.0 5.0 all-reduce.1
  (334 shorter events, 133.3 us)
Async XLA Ops:
  8.0 17.9 %copy-start.31 = (bf16[3,192,192]{2,1,0:T(8,128)(2,1)S(1)}, bf16[3,192,192]{2,1,0:T(8,128)(2,1)}, u32[]{:S(2)}) copy-start(bf16[3,192,192]{2,1,0:T(8,128)(2,1)} %param.20) | copy-start | bytes 663556
  8.0 73.6 %all-gather.8.cloned.1.call-start = ((), (), s32[]{:S(2)}) async-start(), calls=%async_computation.10 | async-start | bytes 2359296 | tf_op jit(solution)/shard_map/all_gather | solution.py:95
  15.2 26.1 %copy-start.32 = (f32[768]{0:T(1024)}, f32[768]{0:T(1024)S(1)}, u32[]{:S(2)}) copy-start(f32[768]{0:T(1024)S(1)} %get-tuple-element.371) | copy-start | bytes 9220
  23.1 18.2 %copy-start.34 = (f32[1,4,2,128]{3,1,2,0:T(4,128)}, f32[1,4,2,128]{3,1,2,0:T(4,128)S(1)}, u32[]{:S(2)}) copy-start(f32[1,4,2,128]{3,1,2,0:T(4,128)S(1)} %copy.135) | copy-start | bytes 12292
  23.1 18.2 %copy-start.3 = (bf16[2,512,768]{2,1,0:T(8,128)(2,1)S(1)}, bf16[2,512,768]{2,1,0:T(8,128)(2,1)}, u32[]{:S(2)}) copy-start(bf16[2,512,768]{2,1,0:T(8,128)(2,1)} %param.16) | copy-start | bytes 4718596
  25.9 16.1 %copy-start.38 = (f32[1024]{0:T(1024)}, f32[1024]{0:T(1024)S(1)}, u32[]{:S(2)}) copy-start(f32[1024]{0:T(1024)S(1)} %rsqrt.21) | copy-start | bytes 12292
  44.3 13.3 %copy-start.37 = (bf16[192,192]{1,0:T(8,128)(2,1)S(1)}, bf16[192,192]{1,0:T(8,128)(2,1)}, u32[]{:S(2)}) copy-start(bf16[192,192]{1,0:T(8,128)(2,1)} %param.22) | copy-start | bytes 221188
  53.0 167.5 %all-reduce.8.cloned.1.call-start = ((), (), s32[]{:S(2)}) async-start(), calls=%async_computation.11 | async-start | bytes 6291456 | tf_op jit(solution)/shard_map/psum | solution.py:33
  65.1 31.8 %copy-start.17 = (bf16[192,768]{0,1:T(8,128)(2,1)}, bf16[192,768]{0,1:T(8,128)(2,1)S(1)}, u32[]{:S(2)}) copy-start(bf16[192,768]{0,1:T(8,128)(2,1)S(1)} %all_gather.49) | copy-start | bytes 884740
  96.9 9.4 copy-start.55
  99.3 127.8 %all-gather.10.cloned.1.call-start = ((), (), s32[]{:S(2)}) async-start(), calls=%async_computation.12 | async-start | bytes 1474560 | tf_op jit(solution)/shard_map/all_gather | solution.py:61
  99.9 132.0 %all-gather.12.cloned.1.call-start = ((), (), s32[]{:S(2)}) async-start(), calls=%async_computation.13 | async-start | bytes 1474560 | tf_op jit(solution)/shard_map/all_gather | solution.py:63
  100.5 262.3 %all-reduce.10.cloned.1.call-start = ((), (), s32[]{:S(2)}) async-start(), calls=%async_computation.14 | async-start | bytes 6291456 | tf_op jit(solution)/shard_map/psum | solution.py:33
  223.3 143.2 %copy-start.1 = (f32[1024,768]{1,0:T(8,128)}, f32[1024,768]{1,0:T(8,128)S(1)}, u32[]{:S(2)}) copy-start(f32[1024,768]{1,0:T(8,128)S(1)} %get-tuple-element.431) | copy-start | bytes 9437188
  242.6 459.3 %reduce-scatter.41.cloned.1.call-start = ((), (), s32[]{:S(2)}) async-start(), calls=%async_computation.22 | async-start | bytes 491520
  371.1 332.5 %reduce-scatter.29.cloned.1.call-start = ((), (), s32[]{:S(2)}) async-start(), calls=%async_computation.16 | async-start | bytes 1474560 | tf_op jit(solution)/shard_map/reduce_scatter | solution.py:301
  376.4 327.2 %reduce-scatter.27.cloned.1.call-start = ((), (), s32[]{:S(2)}) async-start(), calls=%async_computation.15 | async-start | bytes 1474560 | tf_op jit(solution)/shard_map/reduce_scatter | solution.py:295
  381.1 343.8 %reduce-scatter.31.cloned.1.call-start = ((), (), s32[]{:S(2)}) async-start(), calls=%async_computation.17 | async-start | bytes 2359296
  536.6 162.9 %copy-start.12 = (bf16[2,512,768]{2,1,0:T(8,128)(2,1)S(1)}, bf16[2,512,768]{2,1,0:T(8,128)(2,1)}, u32[]{:S(2)}) copy-start(bf16[2,512,768]{2,1,0:T(8,128)(2,1)} %param.27) | copy-start | bytes 4718596
  699.4 197.5 %reduce-scatter.45.cloned.1.call-start = ((), (), s32[]{:S(2)}) async-start(), calls=%async_computation.24 | async-start | bytes 20480
  700.9 196.9 %reduce-scatter.43.cloned.1.call-start = ((), (), s32[]{:S(2)}) async-start(), calls=%async_computation.23 | async-start | bytes 245760
  701.8 196.8 %all-reduce.14.cloned.1.call-start = ((), (), s32[]{:S(2)}) async-start(), calls=%async_computation.26 | async-start | bytes 1376256 | tf_op jit(solution)/shard_map/psum | solution.py:310
  703.6 200.5 %reduce-scatter.39.cloned.1.call-start = ((), (), s32[]{:S(2)}) async-start(), calls=%async_computation.21 | async-start | bytes 20480
  881.9 47.1 %reduce-scatter.37.cloned.1.call-start = ((), (), s32[]{:S(2)}) async-start(), calls=%async_computation.20 | async-start | bytes 1228800
  887.8 232.1 %all-reduce.12.cloned.1.call-start = ((), (), s32[]{:S(2)}) async-start(), calls=%async_computation.25 | async-start | bytes 12582912 | tf_op jit(solution)/shard_map/psum | solution.py:33
  896.8 250.9 %reduce-scatter.33.cloned.1.call-start = ((), (), s32[]{:S(2)}) async-start(), calls=%async_computation.18 | async-start | bytes 245760
  900.2 219.6 %copy-start.4 = (bf16[2,512,768]{2,1,0:T(8,128)(2,1)S(1)}, bf16[2,512,768]{2,1,0:T(8,128)(2,1)}, u32[]{:S(2)}) copy-start(bf16[2,512,768]{2,1,0:T(8,128)(2,1)} %param.16) | copy-start | bytes 4718596
  900.2 219.6 %copy-start.33 = (f32[768]{0:T(1024)S(1)}, f32[768]{0:T(1024)}, u32[]{:S(2)}) copy-start(f32[768]{0:T(1024)} %copy-done.32) | copy-start | bytes 9220
  900.2 219.7 %copy-start.35 = (f32[1,4,2,128]{3,1,2,0:T(4,128)S(1)}, f32[1,4,2,128]{3,1,2,0:T(4,128)}, u32[]{:S(2)}) copy-start(f32[1,4,2,128]{3,1,2,0:T(4,128)} %copy-done.34) | copy-start | bytes 12292
  939.6 183.2 %copy-start.49 = (f32[1,4,2,128]{3,1,2,0:T(4,128)S(1)}, f32[1,4,2,128]{3,1,2,0:T(4,128)}, u32[]{:S(2)}) copy-start(f32[1,4,2,128]{3,1,2,0:T(4,128)} %copy-done.48) | copy-start | bytes 12292
  939.6 183.2 %copy-start.39 = (f32[1024]{0:T(1024)S(1)}, f32[1024]{0:T(1024)}, u32[]{:S(2)}) copy-start(f32[1024]{0:T(1024)} %copy-done.38) | copy-start | bytes 12292
  1129.0 41.1 %reduce-scatter.35.cloned.1.call-start = ((), (), s32[]{:S(2)}) async-start(), calls=%async_computation.19 | async-start | bytes 245760
  (52 other events, 142.0 us)
Sparse Core Ops, SparseCore 0:
  53.1 28.4 all-gather.7
  99.4 121.0 all-reduce.7
  242.7 120.0 all-reduce.9
  704.8 43.3 all-reduce.13
  897.0 222.8 all-reduce.11
Sparse Core Ops, SparseCore 1:
  101.4 17.3 all-gather.9
  120.2 17.2 all-gather.11
  371.2 19.7 reduce-scatter.40
  393.6 25.6 reduce-scatter.28
  421.8 25.5 reduce-scatter.26
  699.5 25.4 reduce-scatter.30
  727.2 19.5 reduce-scatter.44
  749.6 19.7 reduce-scatter.42
  882.0 19.5 reduce-scatter.38
  904.7 24.3 reduce-scatter.36
  1129.0 18.7 reduce-scatter.32
  1150.3 19.8 reduce-scatter.34
